TPU v7x, 256 devices: a whole 4x4x8 slice. The times are simulated.
256 devices in a mesh: cfg: 2 (over y_hi), req: 16 (over z, core), tp: 8 (over y_lo, x).
Axes of the slice: x: 4, y: 4 (y_hi: 2, y_lo: 2; y = y_hi * 2 + y_lo), z: 8, core: 2. Of those that a mesh axis runs over, the one named last changes fastest.
Arguments:
- img_hidden: bfloat16 [2, 8192, 3072], P('cfg', 'req'), may hold values from -0.3125 to 0.3125
- txt_hidden: bfloat16 [2, 2048, 3072], P('cfg', 'req'), may hold values from -6 to 6
- latent: float32 [8192, 64], P(('req', 'tp', 'cfg')), may hold values from -6 to 6
- segment: int32 [8192], P('req'), may hold values from 0 to 3, never falling along the last dimension, each value on 1 to 4096 neighbouring positions
- timestep: int32 [4], replicated, may hold values from 0 to 27
- mod_weight: bfloat16 [256, 5, 3072], P('req'), may hold values from -0.375 to 0.375
- qkv_weight: bfloat16 [3072, 3, 3072], P('req', None, 'tp'), may hold values from -0.109375 to 0.109375
- txt_kv_weight: bfloat16 [3072, 2, 3072], P('req', None, 'tp'), may hold values from -0.109375 to 0.109375
- out_weight: bfloat16 [3072, 3072], P('tp'), may hold values from -0.109375 to 0.109375
- final_weight: bfloat16 [3072, 64], replicated, may hold values from -0.109375 to 0.109375
Outputs:
- guided: float32 [8192, 64], P(('req', 'tp', 'cfg'))
- latent_next: float32 [8192, 64], P(('req', 'tp', 'cfg'))
Inputs may be any that keep to these rules, and one draw needn't show every extreme that they name: `segment`: image rows of one request are consecutive and request numbers never fall along the rows; every one of the 4 requests has 1 to 4096 rows, one exactly 4096.
All inputs are finite; a program needn't handle non-finite values.
Results may differ from a plain program's by a relative error of at most 0.04.
Values may be sent and summed in bfloat16 or wider, within the bound.
A program may use at most 128 MiB of HBM per device.

v0:
```python
import jax
import jax.numpy as jnp
from jax import lax
from jax.sharding import PartitionSpec as P

HD = 128
TEMB = 256
TXT = 512
STEPS = 28


GUIDE_SCALE = 4.0


def swapped(value, axis, stride):
    mask = 2**stride
    pairs = [(source, source ^ mask) for source in range(lax.axis_size(axis))]
    return lax.ppermute(value, axis, pairs)


def sigma_table():
    linear_grid = 1.0 - jnp.arange(STEPS + 1, dtype=jnp.float32) / STEPS
    return 3.0 * linear_grid / (1.0 + 2.0 * linear_grid)


def time_features(sigmas):
    half_width = TEMB // 2
    frequency = jnp.exp(-jnp.log(10000.0) * jnp.arange(half_width, dtype=jnp.float32) / half_width)
    angles = 1000.0 * sigmas[:, None] * frequency[None, :]
    features = jnp.concatenate([jnp.cos(angles), jnp.sin(angles)], axis=1)
    return jax.nn.silu(features).astype(jnp.bfloat16)


def layer_norm(hidden):
    hidden = hidden.astype(jnp.float32)
    center = hidden - jnp.mean(hidden, axis=-1, keepdims=True)
    return center * lax.rsqrt(jnp.mean(center * center, axis=-1, keepdims=True) + 1e-06)


def rms_norm(hidden):
    return (hidden * lax.rsqrt(jnp.mean(hidden * hidden, axis=-1, keepdims=True) + 1e-06)).astype(
        jnp.bfloat16
    )


def select_rows(labels, count, table):
    onehot = (labels[:, None] == jnp.arange(count, dtype=jnp.int32)[None, :]).astype(jnp.float32)
    return jnp.dot(onehot, table, precision=lax.Precision.HIGHEST)


def modulate(hidden, labels, count, shift, scale):
    normed = layer_norm(hidden)
    return (
        normed * (1.0 + select_rows(labels, count, scale)) + select_rows(labels, count, shift)
    ).astype(jnp.bfloat16)


def attend(queries, query_labels, key_values, key_labels, block_rows):
    scale = HD ** (-0.5)
    query_count = queries.shape[0]
    heads = queries.shape[1]
    width = key_values.shape[2]
    blocks = key_values.shape[0] // block_rows
    stacked = key_values.reshape(blocks, block_rows, 2, width)
    label_blocks = key_labels.reshape(blocks, block_rows)
    query_low = jnp.min(query_labels)
    query_high = jnp.max(query_labels)

    def add_block(carry, inputs):
        block, block_labels = inputs

        def compute(sums):
            key_part = block[:, 0].reshape(block_rows, heads, HD)
            value_part = block[:, 1].reshape(block_rows, heads, HD)
            scores = (
                jnp.einsum("qhd,khd->hqk", queries, key_part, preferred_element_type=jnp.float32)
                * scale
            )
            allowed = query_labels[:, None] == block_labels[None, :]
            weights = jnp.where(allowed[None], jnp.exp(scores), 0.0)
            numer = sums[0] + jnp.einsum(
                "hqk,khd->qhd",
                weights.astype(jnp.bfloat16),
                value_part,
                preferred_element_type=jnp.float32,
            )
            denom = sums[1] + jnp.sum(weights, axis=2).T
            return (numer, denom)

        def keep(sums):
            return sums

        touches = (jnp.min(block_labels) <= query_high) & (jnp.max(block_labels) >= query_low)
        return (lax.cond(touches, compute, keep, carry), None)

    start_sums = (
        jnp.zeros((query_count, heads, HD), jnp.float32),
        jnp.zeros((query_count, heads), jnp.float32),
    )
    totals, ignored = lax.scan(add_block, start_sums, (stacked, label_blocks))
    return totals


def per_device(
    img_hidden,
    txt_hidden,
    latent,
    segment,
    timestep,
    mod_weight,
    qkv_weight,
    txt_kv_weight,
    out_weight,
    final_weight,
):
    image = img_hidden[0]
    text = txt_hidden[0]
    image_rows = image.shape[0]
    text_rows = text.shape[0]
    width = image.shape[1]
    requests = timestep.shape[0]
    table = sigma_table()
    sig_now = jnp.take(table, timestep)
    sig_next = jnp.take(table, timestep + 1)
    features = time_features(sig_now)
    shard_rows = mod_weight.shape[0]
    feature_part = lax.dynamic_slice_in_dim(
        features, lax.axis_index("req") * shard_rows, shard_rows, 1
    )
    partial_mod = jnp.dot(
        feature_part, mod_weight.reshape(shard_rows, 5 * width), preferred_element_type=jnp.float32
    )
    modulation = (
        lax.psum(partial_mod.astype(jnp.bfloat16), "req")
        .astype(jnp.float32)
        .reshape(requests, 5, width)
    )
    text_labels = (
        lax.axis_index("req") * text_rows + jnp.arange(text_rows, dtype=jnp.int32)
    ) // TXT
    image_in = modulate(image, segment, requests, modulation[:, 0], modulation[:, 1])
    text_in = modulate(text, text_labels, requests, modulation[:, 3], modulation[:, 4])
    head_width = qkv_weight.shape[2]
    heads = head_width // HD
    pieces = (
        lax.all_gather(qkv_weight, "req", axis=0, tiled=True),
        lax.all_gather(txt_kv_weight, "req", axis=0, tiled=True),
    )
    count = pieces[0].shape[0]
    image_proj = jnp.dot(
        image_in, pieces[0].reshape(count, 3 * head_width), preferred_element_type=jnp.float32
    )
    text_proj = jnp.dot(
        text_in, pieces[1].reshape(count, 2 * head_width), preferred_element_type=jnp.float32
    )
    queries = rms_norm(image_proj[:, :head_width].reshape(image_rows, heads, HD))
    keys = jnp.concatenate(
        [
            rms_norm(image_proj[:, head_width : 2 * head_width].reshape(image_rows, heads, HD)),
            rms_norm(text_proj[:, :head_width].reshape(text_rows, heads, HD)),
        ],
        axis=0,
    )
    values = jnp.concatenate(
        [
            image_proj[:, 2 * head_width :].astype(jnp.bfloat16).reshape(image_rows, heads, HD),
            text_proj[:, head_width:].astype(jnp.bfloat16).reshape(text_rows, heads, HD),
        ],
        axis=0,
    )
    key_count = image_rows + text_rows
    key_values = jnp.stack([keys, values], axis=1).reshape(key_count, 2, head_width)
    key_labels = jnp.concatenate([segment, text_labels], axis=0)
    pieces = (
        lax.all_gather(key_values, "req", axis=0, tiled=True),
        lax.all_gather(key_labels, "req", axis=0, tiled=True),
    )
    numer, denom = attend(queries, segment, pieces[0], pieces[1], key_count)
    numer, denom = (numer, denom)
    attended = (numer / denom[:, :, None]).astype(jnp.bfloat16).reshape(image_rows, head_width)
    out_rows = image_rows // lax.axis_size("tp")
    update = lax.psum_scatter(
        jnp.dot(attended, out_weight, preferred_element_type=jnp.float32).astype(jnp.bfloat16),
        "tp",
        scatter_dimension=0,
        tiled=True,
    ).astype(jnp.float32)
    first_row = lax.axis_index("tp") * out_rows
    own_image = lax.dynamic_slice_in_dim(image, first_row, out_rows, 0)
    own_labels = lax.dynamic_slice_in_dim(segment, first_row, out_rows, 0)
    stream = (
        own_image.astype(jnp.float32) + select_rows(own_labels, requests, modulation[:, 2]) * update
    )
    velocity = jnp.dot(
        layer_norm(stream).astype(jnp.bfloat16), final_weight, preferred_element_type=jnp.float32
    )
    half_rows = out_rows // 2
    half_index = lax.axis_index("cfg")
    kept_velocity = lax.dynamic_slice_in_dim(velocity, half_index * half_rows, half_rows, 0)
    sent_velocity = lax.dynamic_slice_in_dim(velocity, (1 - half_index) * half_rows, half_rows, 0)
    kept_labels = lax.dynamic_slice_in_dim(own_labels, half_index * half_rows, half_rows, 0)
    partner = swapped(sent_velocity, "cfg", 0)
    is_first = half_index == 0
    cond_velocity = jnp.where(is_first, kept_velocity, partner)
    uncond_velocity = jnp.where(is_first, partner, kept_velocity)
    guided = uncond_velocity + GUIDE_SCALE * (cond_velocity - uncond_velocity)
    step_size = select_rows(kept_labels, requests, (sig_next - sig_now)[:, None])[:, 0]
    return (guided, latent + step_size[:, None] * guided)


def solution(mesh):
    return jax.shard_map(
        per_device,
        mesh=mesh,
        in_specs=(
            P("cfg", "req", None),
            P("cfg", "req", None),
            P(("req", "tp", "cfg"), None),
            P("req"),
            P(),
            P("req", None, None),
            P("req", None, "tp"),
            P("req", None, "tp"),
            P("tp", None),
            P(),
        ),
        out_specs=(P(("req", "tp", "cfg"), None), P(("req", "tp", "cfg"), None)),
        check_vma=False,
    )
```

profile of v0, /device:TPU:32, one launch (start us, length us, event | category | flops | bytes accessed | tf_op | source)
XLA Modules:
  0.0 569.5 jit_solution(10982219564804795200)
XLA Ops:
  9.5 1.8 copy.51
  15.7 2.7 convert_reduce_fusion
  19.4 99.9 %all-reduce.2.cloned.1.call-done = bf16[4,5,3072]{2,1,0:T(8,128)(2,1)} async-done(((bf16[4,5,3072]{2,1,0:T(8,128)(2,1)}), bf16[4,5,3072]{2,1,0:T(8,128)(2,1)}) %all-reduce.2.cloned.1.call-update) | async-done | bytes 122896 | tf_op jit(solution)/shard_map/psum | solution.py:134
  119.3 2.2 fusion.71
  124.3 3.1 fusion.21
  127.4 37.6 %all-gather.7.cloned.1.call-done = bf16[3072,2,384]{2,1,0:T(2,128)(2,1)} async-done(((bf16[192,2,384]{2,1,0:T(2,128)(2,1)}), bf16[3072,2,384]{2,1,0:T(2,128)(2,1)}) %all-gather.7.cloned.1.call-update) | async-done | bytes 4718608 | tf_op jit(solution)/shard_map/all_gather | solution.py:147
  164.9 3.1 copy.52
  170.6 44.0 %all-gather.5.cloned.1.call-done = bf16[3072,3,384]{2,0,1:T(8,128)(2,1)} async-done(((bf16[192,3,384]{2,0,1:T(8,128)(2,1)}), bf16[3072,3,384]{2,0,1:T(8,128)(2,1)}) %all-gather.5.cloned.1.call-update) | async-done | bytes 7077904 | tf_op jit(solution)/shard_map/all_gather | solution.py:146
  214.6 10.1 %copy.33 = bf16[3072,3,384]{0,2,1:T(8,128)(2,1)} copy(bf16[3072,3,384]{2,0,1:T(8,128)(2,1)} %all-gather.5.cloned.1.call-done) | data formatting | bytes 14155776 | tf_op jit(solution)/shard_map/all_gather | solution.py:146
  224.7 8.2 %fusion.74 = f32[512,1152]{1,0:T(8,128)S(1)} fusion(bf16[512,3072]{1,0:T(8,128)(2,1)} %fusion.21, bf16[3072,1152]{0,1:T(8,128)(2,1)} %bitcast.112), kind=kOutput, calls=%fused_computation.132 | convolution fusion | flops 3623878656 | bytes 12582912 | tf_op jit(solution)/shard_map/dot_general | solution.py:150
  237.8 1.4 copy.35
  239.2 2.5 fusion.70
  242.9 16.1 %all-gather = s32[16,1,640]{2,1,0:T(1,128)S(1)} all-gather(s32[1,1,640]{2,1,0:T(1,128)S(1)} %reshape.222), channel_id=1, replica_groups=mesh['cfg'=2,'req'=16,'tp'=8] {'req'}, dimensions={0}, use_global_device_ids=true | all-gather | bytes 43520 | tf_op jit(solution)/shard_map/all_gather | solution.py:176
  260.3 1.4 copy.38
  262.9 68.4 %all-gather.9.cloned.1.call-done = bf16[10240,2,384]{2,0,1:T(8,128)(2,1)} async-done(((bf16[640,2,384]{2,0,1:T(8,128)(2,1)}), bf16[10240,2,384]{2,0,1:T(8,128)(2,1)}) %all-gather.9.cloned.1.call-update) | async-done | bytes 15728656 | tf_op jit(solution)/shard_map/all_gather | solution.py:175
  331.3 19.6 %copy.39 = bf16[16,640,2,384]{1,3,2,0:T(8,128)(2,1)} copy(bf16[16,640,2,384]{3,1,0,2:T(8,128)(2,1)} %bitcast.110) | data formatting | bytes 31457280 | tf_op jit(solution)/shard_map/while | solution.py:100
  351.9 120.7 %while.12 = (s32[]{:T(128)}, f32[512,3,128]{2,0,1:T(8,128)}, f32[512,3]{0,1:T(4,128)S(1)}, s32[16,640]{1,0:T(8,128)}, s32[]{:T(128)}, /*index=5*/s32[]{:T(128)},...) while((s32[]{:T(128)}, f32[512,3,128]{2,0,1:T(8,128)}, ...), condition=%wide.region_16.18_spmd, body=%wide.region_10.17_spmd.sunk | while | flops 509740288 | bytes 15768307 | solution.py:100
  355.8 7.3 %conditional.2 = ((f32[512,3,128]{2,0,1:T(8,128)}, f32[512,3]{0,1:T(4,128)S(1)})) conditional(s32[]{:T(128)} %convert_element_type.147, (f32[512,3,128]{2,0,1:T(8,128)}, f32[512,3]{0,1:T(4,128)S(1)}) %tuple.54, (s32[512]{0:T(512)S(1)}, s32[1,640]{1,0:T(1,128)S(1)}, bf16[16,640,2,384]{1,3,2,0:T(8,128)(2,1)}, s32[]{:T(128)}, ...), branch_computations={%region_13.14_spmd, %region_14.16_spmd} | conditional | flops 509739008 | bytes 15762976 | solution.py:94
  357.5 2.2 fusion
  359.7 3.3 fusion.10
  366.9 7.3 %conditional.2 = ((f32[512,3,128]{2,0,1:T(8,128)}, f32[512,3]{0,1:T(4,128)S(1)})) conditional(s32[]{:T(128)} %convert_element_type.147, (f32[512,3,128]{2,0,1:T(8,128)}, f32[512,3]{0,1:T(4,128)S(1)}) %tuple.54, (s32[512]{0:T(512)S(1)}, s32[1,640]{1,0:T(1,128)S(1)}, bf16[16,640,2,384]{1,3,2,0:T(8,128)(2,1)}, s32[]{:T(128)}, ...), branch_computations={%region_13.14_spmd, %region_14.16_spmd} | conditional | flops 509739008 | bytes 15762976 | solution.py:94
  368.6 2.2 fusion
  370.9 3.3 fusion.10
  378.1 7.3 %conditional.2 = ((f32[512,3,128]{2,0,1:T(8,128)}, f32[512,3]{0,1:T(4,128)S(1)})) conditional(s32[]{:T(128)} %convert_element_type.147, (f32[512,3,128]{2,0,1:T(8,128)}, f32[512,3]{0,1:T(4,128)S(1)}) %tuple.54, (s32[512]{0:T(512)S(1)}, s32[1,640]{1,0:T(1,128)S(1)}, bf16[16,640,2,384]{1,3,2,0:T(8,128)(2,1)}, s32[]{:T(128)}, ...), branch_computations={%region_13.14_spmd, %region_14.16_spmd} | conditional | flops 509739008 | bytes 15762976 | solution.py:94
  379.8 2.2 fusion
  382.0 3.3 fusion.10
  389.2 7.3 %conditional.2 = ((f32[512,3,128]{2,0,1:T(8,128)}, f32[512,3]{0,1:T(4,128)S(1)})) conditional(s32[]{:T(128)} %convert_element_type.147, (f32[512,3,128]{2,0,1:T(8,128)}, f32[512,3]{0,1:T(4,128)S(1)}) %tuple.54, (s32[512]{0:T(512)S(1)}, s32[1,640]{1,0:T(1,128)S(1)}, bf16[16,640,2,384]{1,3,2,0:T(8,128)(2,1)}, s32[]{:T(128)}, ...), branch_computations={%region_13.14_spmd, %region_14.16_spmd} | conditional | flops 509739008 | bytes 15762976 | solution.py:94
  390.9 2.2 fusion
  393.2 3.3 fusion.10
  400.4 7.3 %conditional.2 = ((f32[512,3,128]{2,0,1:T(8,128)}, f32[512,3]{0,1:T(4,128)S(1)})) conditional(s32[]{:T(128)} %convert_element_type.147, (f32[512,3,128]{2,0,1:T(8,128)}, f32[512,3]{0,1:T(4,128)S(1)}) %tuple.54, (s32[512]{0:T(512)S(1)}, s32[1,640]{1,0:T(1,128)S(1)}, bf16[16,640,2,384]{1,3,2,0:T(8,128)(2,1)}, s32[]{:T(128)}, ...), branch_computations={%region_13.14_spmd, %region_14.16_spmd} | conditional | flops 509739008 | bytes 15762976 | solution.py:94
  402.1 2.2 fusion
  404.3 3.3 fusion.10
  411.5 7.3 %conditional.2 = ((f32[512,3,128]{2,0,1:T(8,128)}, f32[512,3]{0,1:T(4,128)S(1)})) conditional(s32[]{:T(128)} %convert_element_type.147, (f32[512,3,128]{2,0,1:T(8,128)}, f32[512,3]{0,1:T(4,128)S(1)}) %tuple.54, (s32[512]{0:T(512)S(1)}, s32[1,640]{1,0:T(1,128)S(1)}, bf16[16,640,2,384]{1,3,2,0:T(8,128)(2,1)}, s32[]{:T(128)}, ...), branch_computations={%region_13.14_spmd, %region_14.16_spmd} | conditional | flops 509739008 | bytes 15762976 | solution.py:94
  413.2 2.2 fusion
  415.5 3.3 fusion.10
  422.7 7.3 %conditional.2 = ((f32[512,3,128]{2,0,1:T(8,128)}, f32[512,3]{0,1:T(4,128)S(1)})) conditional(s32[]{:T(128)} %convert_element_type.147, (f32[512,3,128]{2,0,1:T(8,128)}, f32[512,3]{0,1:T(4,128)S(1)}) %tuple.54, (s32[512]{0:T(512)S(1)}, s32[1,640]{1,0:T(1,128)S(1)}, bf16[16,640,2,384]{1,3,2,0:T(8,128)(2,1)}, s32[]{:T(128)}, ...), branch_computations={%region_13.14_spmd, %region_14.16_spmd} | conditional | flops 509739008 | bytes 15762976 | solution.py:94
  424.4 2.2 fusion
  426.6 3.3 fusion.10
  433.9 7.3 %conditional.2 = ((f32[512,3,128]{2,0,1:T(8,128)}, f32[512,3]{0,1:T(4,128)S(1)})) conditional(s32[]{:T(128)} %convert_element_type.147, (f32[512,3,128]{2,0,1:T(8,128)}, f32[512,3]{0,1:T(4,128)S(1)}) %tuple.54, (s32[512]{0:T(512)S(1)}, s32[1,640]{1,0:T(1,128)S(1)}, bf16[16,640,2,384]{1,3,2,0:T(8,128)(2,1)}, s32[]{:T(128)}, ...), branch_computations={%region_13.14_spmd, %region_14.16_spmd} | conditional | flops 509739008 | bytes 15762976 | solution.py:94
  435.5 2.2 fusion
  437.8 3.3 fusion.10
  445.0 1.4 fusion.88
  472.6 1.4 copy.41
  474.1 3.5 convolution_convert_fusion.1
  478.5 76.3 %reduce-scatter.2.cloned.1.call-done = bf16[64,3072]{1,0:T(8,128)(2,1)} async-done(((bf16[512,3072]{1,0:T(8,128)(2,1)}), bf16[64,3072]{1,0:T(8,128)(2,1)}) %reduce-scatter.2.cloned.1.call-update) | async-done | bytes 393232 | tf_op jit(solution)/shard_map/reduce_scatter | solution.py:182
  554.8 1.5 fusion.72
  556.9 2.8 collective-permute-start
  559.9 2.3 collective-permute-done
  (158 shorter events, 58.6 us)
Async XLA Ops:
  7.2 467.0 %copy-start = (bf16[384,3072]{1,0:T(8,128)(2,1)S(1)}, bf16[384,3072]{1,0:T(8,128)(2,1)}, u32[]{:S(2)}) copy-start(bf16[384,3072]{1,0:T(8,128)(2,1)} %param.24) | copy-start | bytes 7077892
  7.2 7.9 %copy-start.3 = (bf16[1,128,3072]{2,1,0:T(8,128)(2,1)S(1)}, bf16[1,128,3072]{2,1,0:T(8,128)(2,1)}, u32[]{:S(2)}) copy-start(bf16[1,128,3072]{2,1,0:T(8,128)(2,1)} %param.17) | copy-start | bytes 2359300
  7.2 112.1 %all-reduce.2.cloned.1.call-start = ((), (), s32[]{:S(2)}) async-start(), calls=%async_computation.1 | async-start | bytes 393216 | tf_op jit(solution)/shard_map/psum | solution.py:134
  8.8 2.6 copy-start.11
  13.5 151.4 %all-gather.7.cloned.1.call-start = ((), (), s32[]{:S(2)}) async-start(), calls=%async_computation.3 | async-start | bytes 5013504 | tf_op jit(solution)/shard_map/all_gather | solution.py:147
  14.3 200.3 %all-gather.5.cloned.1.call-start = ((), (), s32[]{:S(2)}) async-start(), calls=%async_computation.2 | async-start | bytes 7520256 | tf_op jit(solution)/shard_map/all_gather | solution.py:146
  15.0 316.3 %all-gather.9.cloned.1.call-start = ((), (), s32[]{:S(2)}) async-start(), calls=%async_computation.4 | async-start | bytes 16711680 | tf_op jit(solution)/shard_map/all_gather | solution.py:175
  15.1 3.3 copy-start.1
  19.3 103.0 %copy-start.8 = (s32[512]{0:T(512)S(1)}, s32[512]{0:T(512)}, u32[]{:S(2)}) copy-start(s32[512]{0:T(512)} %param.19) | copy-start | bytes 6148
  122.4 1.9 copy-start.2
  232.9 1.4 copy-start.4
  239.2 2.5 copy-start.6
  239.2 2.5 copy-start.7
  242.8 312.0 %reduce-scatter.2.cloned.1.call-start = ((), (), s32[]{:S(2)}) async-start(), calls=%async_computation.5 | async-start | bytes 3538944 | tf_op jit(solution)/shard_map/reduce_scatter | solution.py:182
  477.6 77.1 %copy-start.9 = (bf16[4,1,3072]{2,1,0:T(2,128)(2,1)S(1)}, bf16[4,1,3072]{2,1,0:T(2,128)(2,1)}, u32[]{:S(2)}) copy-start(bf16[4,1,3072]{2,1,0:T(2,128)(2,1)} %get-tuple-element.156) | copy-start | bytes 73732
  477.6 79.0 %copy-start.5 = (bf16[3072,64]{0,1:T(8,128)(2,1)S(1)}, bf16[3072,64]{0,1:T(8,128)(2,1)}, u32[]{:S(2)}) copy-start(bf16[3072,64]{0,1:T(8,128)(2,1)} %param.25) | copy-start | bytes 1179652
  477.6 82.1 %copy-start.12 = (f32[4]{0:T(128)S(1)}, f32[4]{0:T(128)}, u32[]{:S(2)}) copy-start(f32[4]{0:T(128)} %copy-done.11) | copy-start | bytes 52
  477.6 82.1 %copy-start.13 = (s32[4]{0:T(128)S(1)}, s32[4]{0:T(128)}, u32[]{:S(2)}) copy-start(s32[4]{0:T(128)} %param.20) | copy-start | bytes 52
  477.6 84.6 %copy-start.10 = (f32[32,64]{1,0:T(8,128)S(1)}, f32[32,64]{1,0:T(8,128)}, u32[]{:S(2)}) copy-start(f32[32,64]{1,0:T(8,128)} %param.18) | copy-start | bytes 24580
  556.9 5.3 collective-permute-start
Sparse Core Ops, SparseCore 0:
  13.7 105.6 all-reduce.1
  121.3 43.5 all-gather.6
  166.9 47.6 all-gather.4
  242.9 88.3 all-gather.8
  477.8 76.9 reduce-scatter.1
where the time goes:
time: 578 us; the launch traced here: 569 us
  waiting for transfers between devices  330 us (57%)
  matrix products  65.3 us (11%)
  local copies, waits for them, and re-layouts  62.2 us (11%)
  loops' own time  40.9 us (7%)
  other arithmetic  37.8 us (7%)
  blocking collectives  16.1 us (3%)
  between operations  14.1 us (2%)
    psum x1, waiting for transfers between devices, per_device(): lax.psum(partial_mod.astype(jnp.bfloat16), 'req').astype(jnp.float32)  99.9 us
    reduce_scatter x1, waiting for transfers between devices, per_device(): lax.psum_scatter(jnp.dot(attended, out_weight, preferred_element_type=jnp...  76.3 us
    all_gather x1, waiting for transfers between devices, per_device(): lax.all_gather(key_values, 'req', axis=0, tiled=True)  68.4 us
    all_gather x1, waiting for transfers between devices, per_device(): lax.all_gather(qkv_weight, 'req', axis=0, tiled=True)  44 us
    another operation x1, loops' own time, attend(): totals, ignored = lax.scan(add_block, start_sums, (stacked, label_blocks))  40.4 us
    all_gather x1, waiting for transfers between devices, per_device(): lax.all_gather(txt_kv_weight, 'req', axis=0, tiled=True)  37.6 us
    dot_general x8, matrix products, compute(): jnp.einsum('hqk,khd->qhd', weights.astype(jnp.bfloat16), value_part, pref...  26.5 us
    reduce_max x16, other arithmetic, add_block(): jnp.max(block_labels) >= query_low  22.2 us
  transfers between devices with their start and end apart: 6, of which 6 were waited for; matrix products, arithmetic and copies ran while one was open for 4% of the time, Pallas kernels for 0%

commit v1 on v0

v1 whole, which is shorter than its diff:
```python
import functools
import math

import jax
import jax.numpy as jnp
from jax import lax
from jax.experimental import pallas as pl
from jax.experimental.pallas import tpu as pltpu
from jax.sharding import PartitionSpec as P

HD = 128
TEMB = 256
TXT = 512
STEPS = 28
REQS = 4
GUIDE_SCALE = 4.0
MESH = pl.DeviceIdType.MESH
VMEM_LIMIT = 66_000_000


def sigma_table():
    linear_grid = 1.0 - jnp.arange(STEPS + 1, dtype=jnp.float32) / STEPS
    return 3.0 * linear_grid / (1.0 + 2.0 * linear_grid)


def time_features(sigmas):
    half_width = TEMB // 2
    frequency = jnp.exp(-jnp.log(10000.0) * jnp.arange(half_width, dtype=jnp.float32) / half_width)
    angles = 1000.0 * sigmas[:, None] * frequency[None, :]
    features = jnp.concatenate([jnp.cos(angles), jnp.sin(angles)], axis=1)
    return jax.nn.silu(features).astype(jnp.bfloat16)


def rms_heads(value):
    parts = []
    for h in range(value.shape[1] // HD):
        part = value[:, h * HD : (h + 1) * HD]
        mean = jnp.mean(part * part, axis=-1, keepdims=True)
        parts.append((part * lax.rsqrt(mean + 1e-06)).astype(jnp.bfloat16))
    return jnp.concatenate(parts, axis=1)


class Ring:
    def __init__(self, own, held, z, c, chips, sems):
        self.own, self.held, self.z, self.c, self.chips = own, held, z, c, chips
        self.send, self.recv, self.sib_send, self.sib_recv = sems
        self.half = held.shape[1] // 2

    def rows(self, h):
        return pl.ds(h * self.half, self.half)

    def copy(self, d, s, h):
        sign = 1 if d == 0 else -1
        origin = lax.rem(self.z - sign * (s - 1) + self.chips, self.chips)
        target = lax.rem(self.z + sign + self.chips, self.chips)
        slot = self.held.at[2 * origin + self.c, self.rows(h)]
        source = self.own.at[self.rows(h)] if s == 1 else slot
        return pltpu.make_async_remote_copy(
            source,
            slot,
            self.send.at[d, s - 1, h],
            self.recv.at[d, s - 1, h],
            device_id={"req": 2 * target + self.c},
            device_id_type=MESH,
        )

    def arrived(self, d, s, h):
        sign = 1 if d == 0 else -1
        origin = lax.rem(self.z - sign * s + self.chips, self.chips)
        slot = self.held.at[2 * origin + self.c, self.rows(h)]
        return pltpu.make_async_remote_copy(
            slot,
            slot,
            self.send.at[d, s - 1, h],
            self.recv.at[d, s - 1, h],
            device_id={"req": 2 * self.z + 1 - self.c},
            device_id_type=MESH,
        )

    def origin(self, k):
        step = (k + 1) // 2
        sign = 1 if k % 2 == 1 else -1
        return lax.rem(self.z - sign * step + self.chips, self.chips)

    def sibling(self, k, h, core):
        slot = self.held.at[2 * self.origin(k) + core, self.rows(h)]
        source = self.own.at[self.rows(h)] if k == 0 else slot
        return pltpu.make_async_remote_copy(
            source,
            slot,
            self.sib_send.at[k, h],
            self.sib_recv.at[k, h],
            device_id={"req": 2 * self.z + 1 - self.c},
            device_id_type=MESH,
        )

    def start(self):
        for h in range(2):
            for d in range(2):
                self.copy(d, 1, h).start()
        for h in range(2):
            self.sibling(0, h, self.c).start()

    def poll(self, s, h):
        last = self.chips // 2
        for d in range(2):
            if s == last and h != d:
                continue
            self.arrived(d, s, h).wait_recv()
            if s + 1 < last or (s + 1 == last and h == d):
                self.copy(d, s + 1, h).start()
            self.sibling(2 * s - 1 + (d if s < last else 0), h, self.c).start()

    def take(self, k):
        for h in range(2):
            self.sibling(k, h, 1 - self.c).wait_recv()

    def finish(self):
        last = self.chips // 2
        for s in range(1, last + 1):
            for h in range(2):
                for d in range(2):
                    if s < last or h == d:
                        self.copy(d, s, h).wait_send()
        for k in range(self.chips):
            for h in range(2):
                self.sibling(k, h, self.c).wait_send()


def ring_sems(chips):
    return [
        pltpu.SemaphoreType.DMA((2, chips // 2, 2)),
        pltpu.SemaphoreType.DMA((2, chips // 2, 2)),
        pltpu.SemaphoreType.DMA((chips, 2)),
        pltpu.SemaphoreType.DMA((chips, 2)),
    ]


def project_kernel(
    peers,
    w_ref,
    image_ref,
    text_ref,
    label_row_ref,
    label_ref,
    partial_ref,
    q_ref,
    kv_ref,
    labels_ref,
    mod_ref,
    held,
    image,
    text,
    ready,
    text_ready,
    acc,
    text_acc,
    parts,
    mod,
    labels,
    send,
    recv,
    sib_send,
    sib_recv,
    part_send,
    part_recv,
    mod_send,
    mod_recv,
    lab_send,
    lab_recv,
    local,
):
    me = lax.axis_index("req")
    z, c = me // 2, lax.rem(me, 2)
    chips = peers // 2
    rows, width = image.shape
    text_rows = text.shape[0]
    head_width = q_ref.shape[1]
    wide = width // chips

    barrier = pltpu.get_barrier_semaphore()
    for k in range(1, peers):
        pl.semaphore_signal(
            barrier, inc=1, device_id={"req": lax.rem(me + k, peers)}, device_id_type=MESH
        )
    pl.semaphore_wait(barrier, peers - 1)

    ring = Ring(w_ref, held, z, c, chips, (send, recv, sib_send, sib_recv))

    def part_copy(k):
        target = lax.rem(me + k, peers)
        return pltpu.make_async_remote_copy(
            partial_ref.at[target], parts.at[k], part_send.at[k], part_recv.at[k],
            device_id={"req": target}, device_id_type=MESH,
        )

    def mod_copy(k, owner):
        return pltpu.make_async_remote_copy(
            mod.at[owner], mod.at[owner], mod_send.at[k], mod_recv.at[k],
            device_id={"req": lax.rem(me + k, peers)}, device_id_type=MESH,
        )

    def label_copy(k, owner):
        return pltpu.make_async_remote_copy(
            label_row_ref, labels.at[owner], lab_send.at[k], lab_recv.at[k],
            device_id={"req": lax.rem(me + k, peers)}, device_id_type=MESH,
        )

    for k in range(1, peers):
        part_copy(k).start()
    ring.start()
    own_part = pltpu.make_async_copy(partial_ref.at[me], parts.at[0], local.at[0])
    own_part.start()
    image_in = pltpu.make_async_copy(image_ref, image, local.at[1])
    image_in.start()
    text_in = pltpu.make_async_copy(text_ref, text, local.at[2])
    text_in.start()
    own_w = pltpu.make_async_copy(w_ref, held.at[me], local.at[3])
    own_w.start()
    own_label = pltpu.make_async_copy(label_row_ref, labels.at[me], local.at[4])
    own_label.start()
    for k in range(1, peers):
        label_copy(k, me).start()

    own_part.wait()
    for k in range(1, peers):
        part_copy(k).wait_recv()
    total = parts[0]
    for k in range(1, peers):
        total = total + parts[k]
    mod[me] = total
    for k in range(1, peers):
        mod_copy(k, me).start()
    image_in.wait()
    text_in.wait()
    for k in range(1, peers):
        mod_copy(k, lax.rem(me - k + peers, peers)).wait_recv()

    def mod_row(request, component, chunk):
        return mod[2 * chunk + request // 2, 5 * (request % 2) + component : 5 * (request % 2) + component + 1, :]

    tile = 32

    def image_tile(i, carry):
        span = pl.ds(i * tile, tile)
        value = image[span, :].astype(jnp.float32)
        center = value - jnp.mean(value, axis=-1, keepdims=True)
        rstd = lax.rsqrt(jnp.mean(center * center, axis=-1, keepdims=True) + 1e-06)
        label = label_ref[span, :]
        for chunk in range(chips):
            shift = mod_row(REQS - 1, 0, chunk)
            scale = mod_row(REQS - 1, 1, chunk)
            for request in range(REQS - 2, -1, -1):
                mine = label == request
                shift = jnp.where(mine, mod_row(request, 0, chunk), shift)
                scale = jnp.where(mine, mod_row(request, 1, chunk), scale)
            part = center[:, chunk * wide : (chunk + 1) * wide] * rstd
            ready[chunk, span, :] = (part * (1.0 + scale) + shift).astype(jnp.bfloat16)
        return carry

    text_request = me * text_rows // TXT
    text_base = text_request // 2
    text_half = 5 * lax.rem(text_request, 2)

    def text_tile(i, carry):
        span = pl.ds(i * tile, tile)
        value = text[span, :].astype(jnp.float32)
        center = value - jnp.mean(value, axis=-1, keepdims=True)
        rstd = lax.rsqrt(jnp.mean(center * center, axis=-1, keepdims=True) + 1e-06)
        for chunk in range(chips):
            shift = mod[2 * chunk + text_base, pl.ds(text_half + 3, 1), :]
            scale = mod[2 * chunk + text_base, pl.ds(text_half + 4, 1), :]
            part = center[:, chunk * wide : (chunk + 1) * wide] * rstd
            text_ready[chunk, span, :] = (part * (1.0 + scale) + shift).astype(jnp.bfloat16)
        return carry

    image_width = 3 * head_width
    block = w_ref.shape[0]
    mtile = 128

    def multiply(k):
        chip = ring.origin(k)

        def one(i, carry):
            span = pl.ds(i * mtile, mtile)
            lhs = ready[chip, span, :]
            rhs = held[pl.ds(2 * chip, 2), :, :image_width].reshape(2 * block, image_width)
            product = jnp.dot(lhs, rhs, preferred_element_type=jnp.float32)
            acc[span, :] = product if k == 0 else acc[span, :] + product
            return carry

        lax.fori_loop(0, rows // mtile, one, 0)
        text_product = jnp.dot(
            text_ready[chip],
            held[pl.ds(2 * chip, 2), :, image_width:].reshape(2 * block, 2 * head_width),
            preferred_element_type=jnp.float32,
        )
        text_acc[...] = text_product if k == 0 else text_acc[...] + text_product

    lax.fori_loop(0, text_rows // tile, text_tile, 0)
    ring.poll(1, 0)
    lax.fori_loop(0, rows // tile // 2, image_tile, 0)
    ring.poll(1, 1)
    lax.fori_loop(rows // tile // 2, rows // tile, image_tile, 0)
    own_w.wait()
    ring.take(0)
    multiply(0)
    last = chips // 2
    for s in range(2, last + 1):
        ring.poll(s, 0)
        ring.take(2 * s - 3)
        multiply(2 * s - 3)
        ring.poll(s, 1)
        ring.take(2 * s - 2)
        multiply(2 * s - 2)
    ring.take(chips - 1)
    multiply(chips - 1)

    def finish_tile(i, carry):
        span = pl.ds(i * mtile, mtile)
        q_ref[span, :] = rms_heads(acc[span, :head_width])
        kv_ref[span, :head_width] = rms_heads(acc[span, head_width : 2 * head_width])
        kv_ref[span, head_width:] = acc[span, 2 * head_width :].astype(jnp.bfloat16)
        return carry

    lax.fori_loop(0, rows // mtile, finish_tile, 0)
    kv_ref[rows:, :head_width] = rms_heads(text_acc[:, :head_width])
    kv_ref[rows:, head_width:] = text_acc[:, head_width:].astype(jnp.bfloat16)
    own_label.wait()
    for k in range(1, peers):
        label_copy(k, lax.rem(me - k + peers, peers)).wait_recv()
    labels_ref[...] = labels[...]
    mod_ref[...] = mod[...]
    for k in range(1, peers):
        part_copy(k).wait_send()
        mod_copy(k, me).wait_send()
        label_copy(k, me).wait_send()
    ring.finish()


def attend_kernel(
    peers,
    kv_ref,
    out_w_ref,
    image_ref,
    q_ref,
    label_ref,
    labels_ref,
    mod_ref,
    final_ref,
    latent_ref,
    dsig_ref,
    guided_ref,
    next_ref,
    held,
    out_w,
    numer,
    denom,
    attended,
    gathered,
    update,
    image,
    velocity,
    other_velocity,
    send,
    recv,
    sib_send,
    sib_recv,
    x_send,
    x_recv,
    y_send,
    y_recv,
    ws_send,
    ws_recv,
    a_send,
    a_recv,
    v_send,
    v_recv,
    local,
):
    me = lax.axis_index("req")
    tp = lax.axis_index("tp")
    cfg = lax.axis_index("cfg")
    z, c = me // 2, lax.rem(me, 2)
    chips = peers // 2
    y, x = tp // 4, lax.rem(tp, 4)
    rows, head_width = q_ref.shape
    heads = head_width // HD
    block = held.shape[1]
    right = lax.rem(x + 1, 4)
    left = lax.rem(x + 3, 4)
    flip = lax.rem(tp + 4, 8)

    barrier = pltpu.get_barrier_semaphore()
    greet = [
        {"req": 2 * lax.rem(z + 1, chips) + c},
        {"req": 2 * lax.rem(z + chips - 1, chips) + c},
        {"req": 2 * z + 1 - c},
        {"cfg": 1 - cfg, "tp": flip},
        {"cfg": 1 - cfg},
    ] + [{"tp": lax.rem(tp + k, 8)} for k in range(1, 8)]
    for peer in greet:
        pl.semaphore_signal(barrier, inc=1, device_id=peer, device_id_type=MESH)
    pl.semaphore_wait(barrier, len(greet))

    ring = Ring(kv_ref, held, z, c, chips, (send, recv, sib_send, sib_recv))
    ring.start()
    own_kv = pltpu.make_async_copy(kv_ref, held.at[me], local.at[0])
    own_kv.start()

    piece = out_w.shape[1] // 4

    def w_rows(core, h):
        return pl.ds(core * 2 * piece + h * piece, piece)

    def w_copy(source, shard, core, h, sems, index, peer):
        slot = out_w.at[shard, w_rows(core, h)]
        return pltpu.make_async_remote_copy(
            slot if source is None else source,
            slot,
            sems[0].at[index],
            sems[1].at[index],
            device_id=peer,
            device_id_type=MESH,
        )

    xs, ys, ws = (x_send, x_recv), (y_send, y_recv), (ws_send, ws_recv)
    across = [x, left, right, lax.rem(x + 2, 4)]
    to_right, to_left = {"tp": y * 4 + right}, {"tp": y * 4 + left}
    to_y = [{"tp": flip}, {"cfg": 1 - cfg, "tp": flip}]
    to_sibling = {"req": 2 * z + 1 - c}
    own_piece = [out_w_ref.at[w_rows(c, h)] for h in range(2)]

    def x_copy(d, h):
        return w_copy(own_piece[h], tp, c, h, xs, 2 * d + h, to_right if d == 0 else to_left)

    def x_arrived(d, h):
        return w_copy(None, y * 4 + (left if d == 0 else right), c, h, xs, 2 * d + h, to_sibling)

    def x_forward(d):
        return w_copy(None, y * 4 + (left if d == 0 else right), c, d, xs, 4 + d, to_right if d == 0 else to_left)

    def x_forwarded(d):
        return w_copy(None, y * 4 + across[3], c, d, xs, 4 + d, to_sibling)

    def y_copy(n, h):
        return w_copy(own_piece[h] if n == 0 else None, y * 4 + across[n], c, h, ys, 2 * n + h, to_y[h])

    def y_arrived(n, h):
        return w_copy(None, (1 - y) * 4 + across[n], c, h, ys, 2 * n + h, to_sibling)

    def w_sibling(n, h, core):
        shard = y * 4 + across[n] if n < 4 else (1 - y) * 4 + across[n - 4]
        return w_copy(None, shard, core, h, ws, 2 * n + h, to_sibling)

    for h in range(2):
        for d in range(2):
            x_copy(d, h).start()
        y_copy(0, h).start()
    own_out = pltpu.make_async_copy(out_w_ref, out_w.at[tp], local.at[1])
    own_out.start()
    out_rows = rows // 8
    own_image = pltpu.make_async_copy(
        image_ref.at[pl.ds(tp * out_rows, out_rows)], image, local.at[2]
    )
    own_image.start()
    numer[...] = jnp.zeros_like(numer)
    denom[...] = jnp.zeros_like(denom)

    def x_events():
        for h in range(2):
            for d in range(2):
                x_arrived(d, h).wait_recv()
                if h == d:
                    x_forward(d).start()
                y_copy(1 + d, h).start()
                w_sibling(1 + d, h, c).start()

    def x_more():
        for d in range(2):
            x_forwarded(d).wait_recv()
            y_copy(3, d).start()
            w_sibling(3, d, c).start()

    def y_events(n):
        for h in range(2):
            y_arrived(n, h).wait_recv()
            w_sibling(4 + n, h, c).start()

    factor = HD ** (-0.5) * math.log2(math.e)
    qtile = 128
    text_keys = block - rows

    def attend(k):
        chip = ring.origin(k)

        def one(i, carry):
            b = 2 * chip + i // (rows // qtile)
            span = pl.ds(lax.rem(i, rows // qtile) * qtile, qtile)
            text_label = jnp.full((1, text_keys), b * text_keys // TXT, jnp.int32)
            key_label = jnp.concatenate([labels_ref[b], text_label], axis=1)
            allowed = label_ref[span, :] == key_label
            for h in range(heads):
                q = q_ref[span, h * HD : (h + 1) * HD]
                key = held[b, :, h * HD : (h + 1) * HD]
                value = held[b, :, head_width + h * HD : head_width + (h + 1) * HD]
                scores = lax.dot_general(
                    q, key, (((1,), (1,)), ((), ())), preferred_element_type=jnp.float32
                )
                weights = jnp.where(allowed, jnp.exp2(scores * factor), 0.0)
                part = weights[:, :HD]
                for j in range(1, block // HD):
                    part = part + weights[:, j * HD : (j + 1) * HD]
                denom[h, span, :] += part
                numer[h, span, :] += jnp.dot(
                    weights.astype(jnp.bfloat16), value, preferred_element_type=jnp.float32
                )
            return carry

        lax.fori_loop(0, 2 * (rows // qtile), one, 0)

    own_kv.wait()
    ring.take(0)
    attend(0)
    ring.poll(1, 0)
    ring.poll(1, 1)
    last = chips // 2
    for s in range(2, last + 1):
        ring.poll(s, 0)
        if s == 2:
            x_events()
        ring.take(2 * s - 3)
        attend(2 * s - 3)
        if s == 3:
            x_more()
            y_events(0)
        ring.poll(s, 1)
        ring.take(2 * s - 2)
        attend(2 * s - 2)
        if s == 3:
            y_events(1)
            y_events(2)
    y_events(3)
    ring.take(chips - 1)
    attend(chips - 1)

    for h in range(heads):
        total = jnp.sum(denom[h], axis=-1, keepdims=True)
        value = (numer[h] / total).astype(jnp.bfloat16)
        for t in range(8):
            attended[t, :, h * HD : (h + 1) * HD] = value[t * out_rows : (t + 1) * out_rows]

    def a_copy(k, owner):
        target = lax.rem(tp + k, 8)
        return pltpu.make_async_remote_copy(
            attended.at[target], gathered.at[owner], a_send.at[k], a_recv.at[k],
            device_id={"tp": target}, device_id_type=MESH,
        )

    for k in range(1, 8):
        a_copy(k, tp).start()
    gathered[tp] = attended[tp]

    own_out.wait()
    own_image.wait()
    for n in range(1, 8):
        for h in range(2):
            w_sibling(n, h, 1 - c).wait_recv()
    update[...] = jnp.dot(gathered[tp], out_w[tp], preferred_element_type=jnp.float32)
    for k in range(1, 8):
        a_copy(k, lax.rem(tp - k + 8, 8)).wait_recv()

    def add_shard(k, carry):
        t = lax.rem(tp + k, 8)
        update[...] += jnp.dot(gathered[t], out_w[t], preferred_element_type=jnp.float32)
        return carry

    lax.fori_loop(1, 8, add_shard, 0)

    width = update.shape[1]
    wide = width // chips
    label = label_ref[pl.ds(pl.multiple_of(tp * out_rows, out_rows), out_rows), :]
    masks = [label == request for request in range(REQS - 1)]
    mean = jnp.zeros((out_rows, 1), jnp.float32)
    for chunk in range(chips):
        cols = slice(chunk * wide, (chunk + 1) * wide)

        def gate_row(request):
            row = 5 * (request % 2) + 2
            return mod_ref[2 * chunk + request // 2, row : row + 1, :]

        gate = gate_row(REQS - 1)
        for request in range(REQS - 2, -1, -1):
            gate = jnp.where(masks[request], gate_row(request), gate)
        stream = image[:, cols].astype(jnp.float32) + gate * update[:, cols]
        update[:, cols] = stream
        mean = mean + jnp.sum(stream, axis=-1, keepdims=True)
    center = update[...] - mean / width
    normed = center * lax.rsqrt(jnp.mean(center * center, axis=-1, keepdims=True) + 1e-06)
    velocity[...] = jnp.dot(
        normed.astype(jnp.bfloat16), final_ref[...], preferred_element_type=jnp.float32
    )
    half_rows = out_rows // 2
    sent = pl.ds(pl.multiple_of((1 - cfg) * half_rows, half_rows), half_rows)
    kept = pl.ds(pl.multiple_of(cfg * half_rows, half_rows), half_rows)
    swap = pltpu.make_async_remote_copy(
        velocity.at[sent], other_velocity, v_send, v_recv,
        device_id={"cfg": 1 - cfg}, device_id_type=MESH,
    )
    swap.start()
    own = velocity[kept, :]
    own_label = label_ref[pl.ds(pl.multiple_of(tp * out_rows + cfg * half_rows, half_rows), half_rows), :]
    step = jnp.where(
        own_label == 0,
        dsig_ref[0],
        jnp.where(own_label == 1, dsig_ref[1], jnp.where(own_label == 2, dsig_ref[2], dsig_ref[3])),
    )
    swap.wait()
    other = other_velocity[...]
    first = cfg == 0
    cond = jnp.where(first, own, other)
    uncond = jnp.where(first, other, own)
    guided = uncond + GUIDE_SCALE * (cond - uncond)
    guided_ref[...] = guided
    next_ref[...] = latent_ref[...] + step * guided

    for h in range(2):
        for d in range(2):
            x_copy(d, h).wait_send()
    for d in range(2):
        x_forward(d).wait_send()
    for n in range(4):
        for h in range(2):
            y_copy(n, h).wait_send()
    for n in range(1, 8):
        for h in range(2):
            w_sibling(n, h, c).wait_send()
    for k in range(1, 8):
        a_copy(k, tp).wait_send()
    ring.finish()


def per_device(
    peers,
    img_hidden,
    txt_hidden,
    latent,
    segment,
    timestep,
    mod_weight,
    qkv_weight,
    txt_kv_weight,
    out_weight,
    final_weight,
):
    image = img_hidden[0]
    text = txt_hidden[0]
    rows, width = image.shape
    text_rows = text.shape[0]
    shard, comps = mod_weight.shape[:2]
    chips = peers // 2
    wide = width // chips
    head_width = qkv_weight.shape[2]
    block_rows = rows + text_rows
    table = sigma_table()
    sig_now = jnp.take(table, timestep)
    sig_next = jnp.take(table, timestep + 1)
    features = time_features(sig_now)
    feature_part = lax.dynamic_slice_in_dim(features, lax.axis_index("req") * shard, shard, 1)
    partial_mod = jnp.einsum(
        "rj,jkd->rkd", feature_part, mod_weight, preferred_element_type=jnp.float32
    )
    partial_mod = (
        partial_mod.reshape(2, 2 * comps, chips, wide).transpose(2, 0, 1, 3)
    ).reshape(peers, 2 * comps, wide)
    weights = jnp.concatenate(
        [
            qkv_weight.reshape(qkv_weight.shape[0], 3 * head_width),
            txt_kv_weight.reshape(qkv_weight.shape[0], 2 * head_width),
        ],
        axis=1,
    )
    label_row = segment.reshape(1, rows)
    label = segment.reshape(rows, 1)
    any_spec = pl.BlockSpec(memory_space=pl.ANY)
    vmem = pl.BlockSpec(memory_space=pltpu.VMEM)
    dma = pltpu.SemaphoreType.DMA
    queries, key_values, labels, mod = pl.pallas_call(
        functools.partial(project_kernel, peers),
        out_shape=(
            jax.ShapeDtypeStruct((rows, head_width), jnp.bfloat16),
            jax.ShapeDtypeStruct((block_rows, 2 * head_width), jnp.bfloat16),
            jax.ShapeDtypeStruct((peers, 1, rows), jnp.int32),
            jax.ShapeDtypeStruct((peers, 2 * comps, wide), jnp.float32),
        ),
        in_specs=[any_spec, any_spec, any_spec, vmem, vmem, vmem],
        out_specs=(vmem, vmem, vmem, vmem),
        scratch_shapes=[
            pltpu.VMEM((peers, weights.shape[0], weights.shape[1]), jnp.bfloat16),
            pltpu.VMEM((rows, width), jnp.bfloat16),
            pltpu.VMEM((text_rows, width), jnp.bfloat16),
            pltpu.VMEM((chips, rows, wide), jnp.bfloat16),
            pltpu.VMEM((chips, text_rows, wide), jnp.bfloat16),
            pltpu.VMEM((rows, 3 * head_width), jnp.float32),
            pltpu.VMEM((text_rows, 2 * head_width), jnp.float32),
            pltpu.VMEM((peers, 2 * comps, wide), jnp.float32),
            pltpu.VMEM((peers, 2 * comps, wide), jnp.float32),
            pltpu.VMEM((peers, 1, rows), jnp.int32),
            *ring_sems(chips),
            *[dma((peers,)) for _ in range(6)],
            dma((5,)),
        ],
        compiler_params=pltpu.CompilerParams(
            collective_id=0, has_side_effects=True, vmem_limit_bytes=VMEM_LIMIT
        ),
        name="project",
    )(weights, image, text, label_row, label, partial_mod)
    out_rows = rows // 8
    half_rows = out_rows // 2
    return tuple(
        pl.pallas_call(
            functools.partial(attend_kernel, peers),
            out_shape=(
                jax.ShapeDtypeStruct(latent.shape, jnp.float32),
                jax.ShapeDtypeStruct(latent.shape, jnp.float32),
            ),
            in_specs=[any_spec, any_spec, any_spec]
            + [vmem] * 6
            + [pl.BlockSpec(memory_space=pltpu.SMEM)],
            out_specs=(vmem, vmem),
            scratch_shapes=[
                pltpu.VMEM((peers, block_rows, 2 * head_width), jnp.bfloat16),
                pltpu.VMEM((8, head_width, width), jnp.bfloat16),
                pltpu.VMEM((head_width // HD, rows, HD), jnp.float32),
                pltpu.VMEM((head_width // HD, rows, HD), jnp.float32),
                pltpu.VMEM((8, out_rows, head_width), jnp.bfloat16),
                pltpu.VMEM((8, out_rows, head_width), jnp.bfloat16),
                pltpu.VMEM((out_rows, width), jnp.float32),
                pltpu.VMEM((out_rows, width), jnp.bfloat16),
                pltpu.VMEM((out_rows, latent.shape[1]), jnp.float32),
                pltpu.VMEM((half_rows, latent.shape[1]), jnp.float32),
                *ring_sems(chips),
                dma((6,)),
                dma((6,)),
                dma((8,)),
                dma((8,)),
                dma((16,)),
                dma((16,)),
                dma((8,)),
                dma((8,)),
                dma,
                dma,
                dma((3,)),
            ],
            compiler_params=pltpu.CompilerParams(
                collective_id=1, has_side_effects=True, vmem_limit_bytes=VMEM_LIMIT
            ),
            name="attend",
        )(
            key_values,
            out_weight,
            image,
            queries,
            label,
            labels,
            mod,
            final_weight,
            latent,
            sig_next - sig_now,
        )
    )


def solution(mesh):
    return jax.shard_map(
        functools.partial(per_device, mesh.shape["req"]),
        mesh=mesh,
        in_specs=(
            P("cfg", "req", None),
            P("cfg", "req", None),
            P(("req", "tp", "cfg"), None),
            P("req"),
            P(),
            P("req", None, None),
            P("req", None, "tp"),
            P("req", None, "tp"),
            P("tp", None),
            P(),
        ),
        out_specs=(P(("req", "tp", "cfg"), None), P(("req", "tp", "cfg"), None)),
        check_vma=False,
    )
```

time: 578 us -> 225 us (0.39); the launches traced: 569 us -> 223 us
  waiting for transfers between devices: 330 us -> 0 us
  Pallas kernels: 0 us -> 212 us
  matrix products: 65.3 us -> 0.29 us
  local copies, waits for them, and re-layouts: 62.2 us -> 7.1 us
  loops' own time: 40.9 us -> 0 us
  other arithmetic: 37.8 us -> 2.99 us
  blocking collectives: 16.1 us -> 0 us
  between operations: 14.1 us -> 0.73 us
    pallas_call x0 -> x2, Pallas kernels: none -> 212 us  [the longest x1 118 us: per_device(): pl.pallas_call(functools.partial(attend_kernel, peers), out_shape=(jax.Sh...]
    all_gather x3 -> x0, waiting for transfers between devices: 150 us -> none  [the longest x1 68.4 us: per_device(): lax.all_gather(key_values, 'req', axis=0, tiled=True)]
    psum x1 -> x0, waiting for transfers between devices: 99.9 us -> none  [per_device(): lax.psum(partial_mod.astype(jnp.bfloat16), 'req').astype(jnp.float32)]
    reduce_scatter x1 -> x0, waiting for transfers between devices: 76.3 us -> none  [per_device(): lax.psum_scatter(jnp.dot(attended, out_weight, preferred_element_type=jnp...]
    dot_general x27 -> x1, matrix products: 65.3 us -> 0.29 us  [per_device(): jnp.einsum('rj,jkd->rkd', feature_part, mod_weight, preferred_element_typ...]
    another operation x17 -> x0, loops' own time: 40.9 us -> none  [the longest x1 40.4 us: attend(): totals, ignored = lax.scan(add_block, start_sums, (stacked, label_blocks))]
    reduce_max x16 -> x0, other arithmetic: 22.2 us -> none  [add_block(): jnp.max(block_labels) >= query_low]
    while x3 -> x0, local copies, waits for them, and re-layouts: 21.9 us -> none  [attend(): totals, ignored = lax.scan(add_block, start_sums, (stacked, label_blocks))]
  transfers between devices with their start and end apart: 6 -> 0, of which waited for: 6 -> 0; matrix products, arithmetic and copies ran while one was open for 4% -> 0% of each run, Pallas kernels for 0% -> 0%
where the time goes in v1:
time: 225 us; the launch traced here: 223 us
  Pallas kernels  212 us (94%)
  local copies, waits for them, and re-layouts  7.1 us (3%)
  other arithmetic  2.99 us (1%)
    pallas_call x1, Pallas kernels, per_device(): pl.pallas_call(functools.partial(attend_kernel, peers), out_shape=(jax.Sh...  118 us
    pallas_call x1, Pallas kernels, per_device(): pl.pallas_call(functools.partial(project_kernel, peers), out_shape=(jax.S...  93.8 us

profile of v1, /device:TPU:32, one launch (start us, length us, event | category | flops | bytes accessed | tf_op | source)
XLA Modules:
  0.0 222.9 jit_solution(6501265107588805718)
XLA Ops:
  0.6 0.0 copy-start
  0.7 0.7 compare_select_fusion
  1.4 0.6 gather_fusion.1
  2.0 0.0 copy-start.4
  2.0 0.6 gather_fusion
  2.7 0.0 copy-start.3
  2.7 1.2 fusion.5
  3.9 0.1 multiply_cosine_fusion
  4.0 0.0 copy-done
  4.0 0.3 fusion.2
  4.3 0.0 copy-start.1
  4.3 0.2 copy.15
  4.5 0.1 reshape.38
  4.6 0.8 copy.16
  5.4 0.0 copy-done.4
  5.4 0.9 copy.17.label_ref
  6.2 0.0 copy-done.3
  6.3 0.0 copy-done.1
  6.4 0.9 pad_maximum_fusion.w_ref
  7.3 0.0 copy-start.2
  7.3 93.8 %project.1 = (bf16[512,384]{1,0:T(8,128)(2,1)}, bf16[640,768]{1,0:T(8,128)(2,1)}, s32[16,1,512]{2,1,0:T(1,128)}, f32[16,10,384]{2,1,0:T(8,128)}) custom-call(bf16[192,1920]{1,0:T(8,128)(2,1)} %pad_maximum_fusion.w_ref, bf16[512,3072]{1,0:T(8,128)(2,1)} %bitcast.14, bf16[128,3072]{1,0:T(8,128)(2,1)} %bitcast.20, s32[1,512]{1,0:T(1,128)} %bitcast.23, ...), custom_call_target="tpu_custom_call" | custom-call | tf_op jit(solution)/shard_map/project/pallas_call | solution.py:688
  101.1 0.0 copy-done.2
  101.1 1.2 copy.19.final_ref
  102.3 118.0 %attend.1 = (f32[32,64]{1,0:T(8,128)}, f32[32,64]{1,0:T(8,128)}) custom-call(bf16[640,768]{1,0:T(8,128)(2,1)} %get-tuple-element.7.kv_ref, bf16[384,3072]{1,0:T(8,128)(2,1)} %out_w_ref.1, bf16[512,3072]{1,0:T(8,128)(2,1)} %bitcast.15, bf16[512,384]{1,0:T(8,128)(2,1)} %get-tuple-element.8.q_ref, s32[512,1]{1,0:T(8,128)} %copy.17.label_ref, ...), custom_call_target="tpu_custom_call" | custom-call | tf_op jit(solution)/shard_map/attend/pallas_call | solution.py:721
  220.3 1.3 copy.24
  221.6 1.3 copy.25
  (5 shorter events, 0.1 us)
Async XLA Ops:
  0.6 3.4 %copy-start = (bf16[16,5,3072]{2,0,1:T(8,128)(2,1)S(1)}, bf16[16,5,3072]{2,0,1:T(8,128)(2,1)}, u32[]{:S(2)}) copy-start(bf16[16,5,3072]{2,0,1:T(8,128)(2,1)} %param.17) | copy-start | bytes 1474564
  2.0 3.3 %copy-start.4 = (s32[512]{0:T(512)S(1)}, s32[512]{0:T(512)}, u32[]{:S(2)}) copy-start(s32[512]{0:T(512)} %param.15) | copy-start | bytes 6148
  2.7 3.6 %copy-start.3 = (bf16[192,2,384]{2,1,0:T(2,128)(2,1)S(1)}, bf16[192,2,384]{2,1,0:T(2,128)(2,1)}, u32[]{:S(2)}) copy-start(bf16[192,2,384]{2,1,0:T(2,128)(2,1)} %param.19) | copy-start | bytes 884740
  4.3 2.0 copy-start.1
  7.3 93.8 %copy-start.2 = (bf16[3072,64]{0,1:T(8,128)(2,1)S(1)}, bf16[3072,64]{0,1:T(8,128)(2,1)}, u32[]{:S(2)}) copy-start(bf16[3072,64]{0,1:T(8,128)(2,1)} %param.21) | copy-start | bytes 1179652

commit v2 on v1

--- a/solution.py
+++ b/solution.py
@@ -16,6 +16,7 @@
 GUIDE_SCALE = 4.0
 MESH = pl.DeviceIdType.MESH
 VMEM_LIMIT = 66_000_000
+LEAD = 32
 
 
 def sigma_table():
@@ -41,13 +42,55 @@
 
 
 class Ring:
-    def __init__(self, own, held, z, c, chips, sems):
+    def __init__(self, own, held, z, c, chips, sems, lead=0, cfg=0, pair_sems=None, first=None):
         self.own, self.held, self.z, self.c, self.chips = own, held, z, c, chips
         self.send, self.recv, self.sib_send, self.sib_recv = sems
         self.half = held.shape[1] // 2
+        self.first = self.half if first is None else first
+        self.lead, self.cfg, self.pair_sems = lead, cfg, pair_sems
+
+    def whole(self, h):
+        return pl.ds(0, self.first) if h == 0 else pl.ds(self.first, 2 * self.half - self.first)
 
     def rows(self, h):
-        return pl.ds(h * self.half, self.half)
+        if not self.lead:
+            return self.whole(h)
+        start = pl.multiple_of(h * self.half + self.lead * self.cfg, self.lead)
+        return pl.ds(start, self.half - self.lead)
+
+    def pair_rows(self, h, cfg):
+        start = pl.multiple_of(h * self.half + (self.half - self.lead) * cfg, self.lead)
+        return pl.ds(start, self.lead)
+
+    def pair(self, k, h, cfg):
+        slot = self.held.at[2 * self.origin(k) + self.c, self.pair_rows(h, cfg)]
+        return pltpu.make_async_remote_copy(
+            slot,
+            slot,
+            self.pair_sems[0].at[k, h],
+            self.pair_sems[1].at[k, h],
+            device_id={"cfg": 1 - self.cfg},
+            device_id_type=MESH,
+        )
+
+    def pair_sibling(self, k, h, core):
+        slot = self.held.at[2 * self.origin(k) + core, self.pair_rows(h, 1 - self.cfg)]
+        return pltpu.make_async_remote_copy(
+            slot,
+            slot,
+            self.pair_sems[2].at[k, h],
+            self.pair_sems[3].at[k, h],
+            device_id={"req": 2 * self.z + 1 - self.c},
+            device_id_type=MESH,
+        )
+
+    def chunks(self, s, h):
+        return [2 * s - 1, 2 * s] if s < self.chips // 2 else [2 * s - 1]
+
+    def relay(self, s, h):
+        for k in self.chunks(s, h):
+            self.pair(k, h, 1 - self.cfg).wait_recv()
+            self.pair_sibling(k, h, self.c).start()
 
     def copy(self, d, s, h):
         sign = 1 if d == 0 else -1
@@ -83,8 +126,9 @@
         return lax.rem(self.z - sign * step + self.chips, self.chips)
 
     def sibling(self, k, h, core):
-        slot = self.held.at[2 * self.origin(k) + core, self.rows(h)]
-        source = self.own.at[self.rows(h)] if k == 0 else slot
+        rows = self.whole(h) if k == 0 else self.rows(h)
+        slot = self.held.at[2 * self.origin(k) + core, rows]
+        source = self.own.at[rows] if k == 0 else slot
         return pltpu.make_async_remote_copy(
             source,
             slot,
@@ -109,11 +153,19 @@
             self.arrived(d, s, h).wait_recv()
             if s + 1 < last or (s + 1 == last and h == d):
                 self.copy(d, s + 1, h).start()
-            self.sibling(2 * s - 1 + (d if s < last else 0), h, self.c).start()
+            k = 2 * s - 1 + (d if s < last else 0)
+            if self.lead:
+                self.pair(k, h, self.cfg).start()
+            self.sibling(k, h, self.c).start()
 
     def take(self, k):
         for h in range(2):
-            self.sibling(k, h, 1 - self.c).wait_recv()
+            self.take_half(k, h)
+
+    def take_half(self, k, h):
+        self.sibling(k, h, 1 - self.c).wait_recv()
+        if self.lead and k:
+            self.pair_sibling(k, h, 1 - self.c).wait_recv()
 
     def finish(self):
         last = self.chips // 2
@@ -125,6 +177,9 @@
         for k in range(self.chips):
             for h in range(2):
                 self.sibling(k, h, self.c).wait_send()
+                if self.lead and k:
+                    self.pair(k, h, self.cfg).wait_send()
+                    self.pair_sibling(k, h, self.c).wait_send()
 
 
 def ring_sems(chips):
@@ -162,6 +217,10 @@
     recv,
     sib_send,
     sib_recv,
+    pair_send,
+    pair_recv,
+    pair_sib_send,
+    pair_sib_recv,
     part_send,
     part_recv,
     mod_send,
@@ -171,6 +230,7 @@
     local,
 ):
     me = lax.axis_index("req")
+    plane = 2 * lax.axis_index("tp") + lax.axis_index("cfg")
     z, c = me // 2, lax.rem(me, 2)
     chips = peers // 2
     rows, width = image.shape
@@ -178,26 +238,32 @@
     head_width = q_ref.shape[1]
     wide = width // chips
 
+    def in_plane(k):
+        target = lax.rem(plane + k, peers)
+        return {"tp": target // 2, "cfg": lax.rem(target, 2)}
+
     barrier = pltpu.get_barrier_semaphore()
     for k in range(1, peers):
-        pl.semaphore_signal(
-            barrier, inc=1, device_id={"req": lax.rem(me + k, peers)}, device_id_type=MESH
-        )
-    pl.semaphore_wait(barrier, peers - 1)
-
-    ring = Ring(w_ref, held, z, c, chips, (send, recv, sib_send, sib_recv))
+        for peer in ({"req": lax.rem(me + k, peers)}, in_plane(k)):
+            pl.semaphore_signal(barrier, inc=1, device_id=peer, device_id_type=MESH)
+    pl.semaphore_wait(barrier, 2 * (peers - 1))
+
+    ring = Ring(
+        w_ref, held, z, c, chips, (send, recv, sib_send, sib_recv), LEAD, lax.axis_index("cfg"),
+        (pair_send, pair_recv, pair_sib_send, pair_sib_recv),
+    )
 
     def part_copy(k):
         target = lax.rem(me + k, peers)
         return pltpu.make_async_remote_copy(
-            partial_ref.at[target], parts.at[k], part_send.at[k], part_recv.at[k],
+            partial_ref.at[plane], parts.at[k], part_send.at[k], part_recv.at[k],
             device_id={"req": target}, device_id_type=MESH,
         )
 
     def mod_copy(k, owner):
         return pltpu.make_async_remote_copy(
             mod.at[owner], mod.at[owner], mod_send.at[k], mod_recv.at[k],
-            device_id={"req": lax.rem(me + k, peers)}, device_id_type=MESH,
+            device_id=in_plane(k), device_id_type=MESH,
         )
 
     def label_copy(k, owner):
@@ -209,7 +275,7 @@
     for k in range(1, peers):
         part_copy(k).start()
     ring.start()
-    own_part = pltpu.make_async_copy(partial_ref.at[me], parts.at[0], local.at[0])
+    own_part = pltpu.make_async_copy(partial_ref.at[plane], parts.at[0], local.at[0])
     own_part.start()
     image_in = pltpu.make_async_copy(image_ref, image, local.at[1])
     image_in.start()
@@ -228,13 +294,13 @@
     total = parts[0]
     for k in range(1, peers):
         total = total + parts[k]
-    mod[me] = total
+    mod[plane] = total
     for k in range(1, peers):
-        mod_copy(k, me).start()
+        mod_copy(k, plane).start()
     image_in.wait()
     text_in.wait()
     for k in range(1, peers):
-        mod_copy(k, lax.rem(me - k + peers, peers)).wait_recv()
+        mod_copy(k, lax.rem(plane - k + peers, peers)).wait_recv()
 
     def mod_row(request, component, chunk):
         return mod[2 * chunk + request // 2, 5 * (request % 2) + component : 5 * (request % 2) + component + 1, :]
@@ -276,7 +342,7 @@
 
     image_width = 3 * head_width
     block = w_ref.shape[0]
-    mtile = 128
+    mtile = 256
 
     def multiply(k):
         chip = ring.origin(k)
@@ -308,11 +374,16 @@
     last = chips // 2
     for s in range(2, last + 1):
         ring.poll(s, 0)
+        if s == 2:
+            ring.relay(1, 0)
+        ring.relay(s - 1, 1)
         ring.take(2 * s - 3)
         multiply(2 * s - 3)
         ring.poll(s, 1)
+        ring.relay(s, 0)
         ring.take(2 * s - 2)
         multiply(2 * s - 2)
+    ring.relay(last, 1)
     ring.take(chips - 1)
     multiply(chips - 1)
 
@@ -333,7 +404,7 @@
     mod_ref[...] = mod[...]
     for k in range(1, peers):
         part_copy(k).wait_send()
-        mod_copy(k, me).wait_send()
+        mod_copy(k, plane).wait_send()
         label_copy(k, me).wait_send()
     ring.finish()
 
@@ -403,7 +474,9 @@
         pl.semaphore_signal(barrier, inc=1, device_id=peer, device_id_type=MESH)
     pl.semaphore_wait(barrier, len(greet))
 
-    ring = Ring(kv_ref, held, z, c, chips, (send, recv, sib_send, sib_recv))
+    text_keys = block - rows
+    first = 3 * HD
+    ring = Ring(kv_ref, held, z, c, chips, (send, recv, sib_send, sib_recv), first=first)
     ring.start()
     own_kv = pltpu.make_async_copy(kv_ref, held.at[me], local.at[0])
     own_kv.start()
@@ -488,28 +561,31 @@
             w_sibling(4 + n, h, c).start()
 
     factor = HD ** (-0.5) * math.log2(math.e)
-    qtile = 128
-    text_keys = block - rows
-
-    def attend(k):
+    qtile = 256
+
+    def attend(k, part_of):
         chip = ring.origin(k)
+        keys = slice(0, first) if part_of == 0 else slice(first, block)
 
         def one(i, carry):
             b = 2 * chip + i // (rows // qtile)
             span = pl.ds(lax.rem(i, rows // qtile) * qtile, qtile)
-            text_label = jnp.full((1, text_keys), b * text_keys // TXT, jnp.int32)
-            key_label = jnp.concatenate([labels_ref[b], text_label], axis=1)
+            if part_of == 0:
+                key_label = labels_ref[b, :, keys]
+            else:
+                text_label = jnp.full((1, text_keys), b * text_keys // TXT, jnp.int32)
+                key_label = jnp.concatenate([labels_ref[b, :, first:], text_label], axis=1)
             allowed = label_ref[span, :] == key_label
             for h in range(heads):
                 q = q_ref[span, h * HD : (h + 1) * HD]
-                key = held[b, :, h * HD : (h + 1) * HD]
-                value = held[b, :, head_width + h * HD : head_width + (h + 1) * HD]
+                key = held[b, keys, h * HD : (h + 1) * HD]
+                value = held[b, keys, head_width + h * HD : head_width + (h + 1) * HD]
                 scores = lax.dot_general(
                     q, key, (((1,), (1,)), ((), ())), preferred_element_type=jnp.float32
                 )
                 weights = jnp.where(allowed, jnp.exp2(scores * factor), 0.0)
                 part = weights[:, :HD]
-                for j in range(1, block // HD):
+                for j in range(1, (keys.stop - keys.start) // HD):
                     part = part + weights[:, j * HD : (j + 1) * HD]
                 denom[h, span, :] += part
                 numer[h, span, :] += jnp.dot(
@@ -519,30 +595,39 @@
 
         lax.fori_loop(0, 2 * (rows // qtile), one, 0)
 
+    def attend_halves(s, part_of):
+        for k in ring.chunks(s, part_of):
+            ring.take_half(k, part_of)
+            attend(k, part_of)
+
+    last = chips // 2
     own_kv.wait()
-    ring.take(0)
-    attend(0)
+    ring.take_half(0, 0)
+    attend(0, 0)
     ring.poll(1, 0)
+    ring.take_half(0, 1)
+    attend(0, 1)
     ring.poll(1, 1)
-    last = chips // 2
-    for s in range(2, last + 1):
+    attend_halves(1, 0)
+    for s in range(2, last):
         ring.poll(s, 0)
         if s == 2:
             x_events()
-        ring.take(2 * s - 3)
-        attend(2 * s - 3)
+        attend_halves(s - 1, 1)
         if s == 3:
             x_more()
             y_events(0)
         ring.poll(s, 1)
-        ring.take(2 * s - 2)
-        attend(2 * s - 2)
+        attend_halves(s, 0)
         if s == 3:
             y_events(1)
-            y_events(2)
+    ring.poll(last, 0)
+    attend_halves(last - 1, 1)
+    y_events(2)
+    attend_halves(last, 0)
+    ring.poll(last, 1)
     y_events(3)
-    ring.take(chips - 1)
-    attend(chips - 1)
+    attend_halves(last, 1)
 
     for h in range(heads):
         total = jnp.sum(denom[h], axis=-1, keepdims=True)
@@ -707,6 +792,7 @@
             pltpu.VMEM((peers, 2 * comps, wide), jnp.float32),
             pltpu.VMEM((peers, 1, rows), jnp.int32),
             *ring_sems(chips),
+            *[dma((chips, 2)) for _ in range(4)],
             *[dma((peers,)) for _ in range(6)],
             dma((5,)),
         ],

time: 225 us -> 201 us (0.89)
  Pallas kernels: 212 us -> 189 us
    pallas_call x1, Pallas kernels: 93.8 us -> 76 us  [per_device(): pl.pallas_call(functools.partial(project_kernel, peers), out_shape=(jax.S...]
    pallas_call x1, Pallas kernels: 118 us -> 113 us  [per_device(): pl.pallas_call(functools.partial(attend_kernel, peers), out_shape=(jax.Sh...]
where the time goes in v2:
time: 201 us; the launch traced here: 200 us
  Pallas kernels  189 us (94%)
  local copies, waits for them, and re-layouts  7.1 us (4%)
  other arithmetic  2.99 us (1%)
    pallas_call x1, Pallas kernels, per_device(): pl.pallas_call(functools.partial(attend_kernel, peers), out_shape=(jax.Sh...  113 us
    pallas_call x1, Pallas kernels, per_device(): pl.pallas_call(functools.partial(project_kernel, peers), out_shape=(jax.S...  76 us

profile of v2, /device:TPU:32, one launch (start us, length us, event | category | flops | bytes accessed | tf_op | source)
XLA Modules:
  0.0 199.9 jit_solution(1153322752094547209)
XLA Ops:
  0.6 0.0 copy-start
  0.7 0.7 compare_select_fusion
  1.4 0.6 gather_fusion.1
  2.0 0.0 copy-start.4
  2.0 0.6 gather_fusion
  2.7 0.0 copy-start.3
  2.7 1.2 fusion.5
  3.9 0.1 multiply_cosine_fusion
  4.0 0.0 copy-done
  4.0 0.3 fusion.2
  4.3 0.0 copy-start.1
  4.3 0.2 copy.15
  4.5 0.1 reshape.38
  4.6 0.8 copy.16
  5.4 0.0 copy-done.4
  5.4 0.9 copy.17.label_ref
  6.2 0.0 copy-done.3
  6.3 0.0 copy-done.1
  6.4 0.9 pad_maximum_fusion.w_ref
  7.3 0.0 copy-start.2
  7.3 76.0 %project.1 = (bf16[512,384]{1,0:T(8,128)(2,1)}, bf16[640,768]{1,0:T(8,128)(2,1)}, s32[16,1,512]{2,1,0:T(1,128)}, f32[16,10,384]{2,1,0:T(8,128)}) custom-call(bf16[192,1920]{1,0:T(8,128)(2,1)} %pad_maximum_fusion.w_ref, bf16[512,3072]{1,0:T(8,128)(2,1)} %bitcast.14, bf16[128,3072]{1,0:T(8,128)(2,1)} %bitcast.20, s32[1,512]{1,0:T(1,128)} %bitcast.23, ...), custom_call_target="tpu_custom_call" | custom-call | tf_op jit(solution)/shard_map/project/pallas_call | solution.py:773
  83.3 0.0 copy-done.2
  83.3 1.2 copy.19.final_ref
  84.5 112.8 %attend.1 = (f32[32,64]{1,0:T(8,128)}, f32[32,64]{1,0:T(8,128)}) custom-call(bf16[640,768]{1,0:T(8,128)(2,1)} %get-tuple-element.7.kv_ref, bf16[384,3072]{1,0:T(8,128)(2,1)} %out_w_ref.1, bf16[512,3072]{1,0:T(8,128)(2,1)} %bitcast.15, bf16[512,384]{1,0:T(8,128)(2,1)} %get-tuple-element.8.q_ref, s32[512,1]{1,0:T(8,128)} %copy.17.label_ref, ...), custom_call_target="tpu_custom_call" | custom-call | tf_op jit(solution)/shard_map/attend/pallas_call | solution.py:807
  197.3 1.3 copy.24
  198.6 1.3 copy.25
  (5 shorter events, 0.1 us)
Async XLA Ops:
  0.6 3.4 %copy-start = (bf16[16,5,3072]{2,0,1:T(8,128)(2,1)S(1)}, bf16[16,5,3072]{2,0,1:T(8,128)(2,1)}, u32[]{:S(2)}) copy-start(bf16[16,5,3072]{2,0,1:T(8,128)(2,1)} %param.17) | copy-start | bytes 1474564
  2.0 3.3 %copy-start.4 = (s32[512]{0:T(512)S(1)}, s32[512]{0:T(512)}, u32[]{:S(2)}) copy-start(s32[512]{0:T(512)} %param.15) | copy-start | bytes 6148
  2.7 3.6 %copy-start.3 = (bf16[192,2,384]{2,1,0:T(2,128)(2,1)S(1)}, bf16[192,2,384]{2,1,0:T(2,128)(2,1)}, u32[]{:S(2)}) copy-start(bf16[192,2,384]{2,1,0:T(2,128)(2,1)} %param.19) | copy-start | bytes 884740
  4.3 2.0 copy-start.1
  7.3 76.0 %copy-start.2 = (bf16[3072,64]{0,1:T(8,128)(2,1)S(1)}, bf16[3072,64]{0,1:T(8,128)(2,1)}, u32[]{:S(2)}) copy-start(bf16[3072,64]{0,1:T(8,128)(2,1)} %param.21) | copy-start | bytes 1179652

commit v3 on v2

--- a/solution.py
+++ b/solution.py
@@ -19,9 +19,9 @@
 LEAD = 32
 
 
-def sigma_table():
-    linear_grid = 1.0 - jnp.arange(STEPS + 1, dtype=jnp.float32) / STEPS
-    return 3.0 * linear_grid / (1.0 + 2.0 * linear_grid)
+def sigma(index):
+    linear = 1.0 - index.astype(jnp.float32) / STEPS
+    return 3.0 * linear / (1.0 + 2.0 * linear)
 
 
 def time_features(sigmas):
@@ -42,19 +42,15 @@
 
 
 class Ring:
-    def __init__(self, own, held, z, c, chips, sems, lead=0, cfg=0, pair_sems=None, first=None):
+    def __init__(self, own, held, z, c, chips, sems, lead=0, cfg=0, pair_sems=None):
         self.own, self.held, self.z, self.c, self.chips = own, held, z, c, chips
         self.send, self.recv, self.sib_send, self.sib_recv = sems
         self.half = held.shape[1] // 2
-        self.first = self.half if first is None else first
         self.lead, self.cfg, self.pair_sems = lead, cfg, pair_sems
-
-    def whole(self, h):
-        return pl.ds(0, self.first) if h == 0 else pl.ds(self.first, 2 * self.half - self.first)
 
     def rows(self, h):
         if not self.lead:
-            return self.whole(h)
+            return pl.ds(h * self.half, self.half)
         start = pl.multiple_of(h * self.half + self.lead * self.cfg, self.lead)
         return pl.ds(start, self.half - self.lead)
 
@@ -126,7 +122,7 @@
         return lax.rem(self.z - sign * step + self.chips, self.chips)
 
     def sibling(self, k, h, core):
-        rows = self.whole(h) if k == 0 else self.rows(h)
+        rows = pl.ds(h * self.half, self.half) if k == 0 else self.rows(h)
         slot = self.held.at[2 * self.origin(k) + core, rows]
         source = self.own.at[rows] if k == 0 else slot
         return pltpu.make_async_remote_copy(
@@ -160,12 +156,9 @@
 
     def take(self, k):
         for h in range(2):
-            self.take_half(k, h)
-
-    def take_half(self, k, h):
-        self.sibling(k, h, 1 - self.c).wait_recv()
-        if self.lead and k:
-            self.pair_sibling(k, h, 1 - self.c).wait_recv()
+            self.sibling(k, h, 1 - self.c).wait_recv()
+            if self.lead and k:
+                self.pair_sibling(k, h, 1 - self.c).wait_recv()
 
     def finish(self):
         last = self.chips // 2
@@ -474,9 +467,7 @@
         pl.semaphore_signal(barrier, inc=1, device_id=peer, device_id_type=MESH)
     pl.semaphore_wait(barrier, len(greet))
 
-    text_keys = block - rows
-    first = 3 * HD
-    ring = Ring(kv_ref, held, z, c, chips, (send, recv, sib_send, sib_recv), first=first)
+    ring = Ring(kv_ref, held, z, c, chips, (send, recv, sib_send, sib_recv))
     ring.start()
     own_kv = pltpu.make_async_copy(kv_ref, held.at[me], local.at[0])
     own_kv.start()
@@ -562,30 +553,27 @@
 
     factor = HD ** (-0.5) * math.log2(math.e)
     qtile = 256
-
-    def attend(k, part_of):
+    text_keys = block - rows
+
+    def attend(k):
         chip = ring.origin(k)
-        keys = slice(0, first) if part_of == 0 else slice(first, block)
 
         def one(i, carry):
             b = 2 * chip + i // (rows // qtile)
             span = pl.ds(lax.rem(i, rows // qtile) * qtile, qtile)
-            if part_of == 0:
-                key_label = labels_ref[b, :, keys]
-            else:
-                text_label = jnp.full((1, text_keys), b * text_keys // TXT, jnp.int32)
-                key_label = jnp.concatenate([labels_ref[b, :, first:], text_label], axis=1)
+            text_label = jnp.full((1, text_keys), b * text_keys // TXT, jnp.int32)
+            key_label = jnp.concatenate([labels_ref[b], text_label], axis=1)
             allowed = label_ref[span, :] == key_label
             for h in range(heads):
                 q = q_ref[span, h * HD : (h + 1) * HD]
-                key = held[b, keys, h * HD : (h + 1) * HD]
-                value = held[b, keys, head_width + h * HD : head_width + (h + 1) * HD]
+                key = held[b, :, h * HD : (h + 1) * HD]
+                value = held[b, :, head_width + h * HD : head_width + (h + 1) * HD]
                 scores = lax.dot_general(
                     q, key, (((1,), (1,)), ((), ())), preferred_element_type=jnp.float32
                 )
                 weights = jnp.where(allowed, jnp.exp2(scores * factor), 0.0)
                 part = weights[:, :HD]
-                for j in range(1, (keys.stop - keys.start) // HD):
+                for j in range(1, block // HD):
                     part = part + weights[:, j * HD : (j + 1) * HD]
                 denom[h, span, :] += part
                 numer[h, span, :] += jnp.dot(
@@ -595,39 +583,36 @@
 
         lax.fori_loop(0, 2 * (rows // qtile), one, 0)
 
-    def attend_halves(s, part_of):
-        for k in ring.chunks(s, part_of):
-            ring.take_half(k, part_of)
-            attend(k, part_of)
-
+    own_kv.wait()
+    ring.take(0)
+    attend(0)
+    ring.poll(1, 0)
+    ring.poll(1, 1)
     last = chips // 2
-    own_kv.wait()
-    ring.take_half(0, 0)
-    attend(0, 0)
-    ring.poll(1, 0)
-    ring.take_half(0, 1)
-    attend(0, 1)
-    ring.poll(1, 1)
-    attend_halves(1, 0)
     for s in range(2, last):
         ring.poll(s, 0)
         if s == 2:
             x_events()
-        attend_halves(s - 1, 1)
+        ring.take(2 * s - 3)
+        attend(2 * s - 3)
         if s == 3:
             x_more()
             y_events(0)
         ring.poll(s, 1)
-        attend_halves(s, 0)
+        ring.take(2 * s - 2)
+        attend(2 * s - 2)
         if s == 3:
             y_events(1)
+            y_events(2)
+    ring.take(chips - 3)
+    attend(chips - 3)
     ring.poll(last, 0)
-    attend_halves(last - 1, 1)
-    y_events(2)
-    attend_halves(last, 0)
+    ring.take(chips - 2)
+    attend(chips - 2)
     ring.poll(last, 1)
     y_events(3)
-    attend_halves(last, 1)
+    ring.take(chips - 1)
+    attend(chips - 1)
 
     for h in range(heads):
         total = jnp.sum(denom[h], axis=-1, keepdims=True)
@@ -682,8 +667,9 @@
         mean = mean + jnp.sum(stream, axis=-1, keepdims=True)
     center = update[...] - mean / width
     normed = center * lax.rsqrt(jnp.mean(center * center, axis=-1, keepdims=True) + 1e-06)
-    velocity[...] = jnp.dot(
-        normed.astype(jnp.bfloat16), final_ref[...], preferred_element_type=jnp.float32
+    velocity[...] = lax.dot_general(
+        normed.astype(jnp.bfloat16), final_ref[...], (((1,), (1,)), ((), ())),
+        preferred_element_type=jnp.float32,
     )
     half_rows = out_rows // 2
     sent = pl.ds(pl.multiple_of((1 - cfg) * half_rows, half_rows), half_rows)
@@ -747,9 +733,8 @@
     wide = width // chips
     head_width = qkv_weight.shape[2]
     block_rows = rows + text_rows
-    table = sigma_table()
-    sig_now = jnp.take(table, timestep)
-    sig_next = jnp.take(table, timestep + 1)
+    sig_now = sigma(timestep)
+    sig_next = sigma(timestep + 1)
     features = time_features(sig_now)
     feature_part = lax.dynamic_slice_in_dim(features, lax.axis_index("req") * shard, shard, 1)
     partial_mod = jnp.einsum(
@@ -850,7 +835,7 @@
             label,
             labels,
             mod,
-            final_weight,
+            final_weight.T,
             latent,
             sig_next - sig_now,
         )

time: 201 us -> 193 us (0.960)
  Pallas kernels: 189 us -> 184 us
  local copies, waits for them, and re-layouts: 7.1 us -> 4.66 us
    pallas_call x1, Pallas kernels: 113 us -> 108 us  [per_device(): pl.pallas_call(functools.partial(attend_kernel, peers), out_shape=(jax.Sh...]
where the time goes in v3:
time: 193 us; the launch traced here: 192 us
  Pallas kernels  184 us (95%)
  local copies, waits for them, and re-layouts  4.66 us (2%)
  other arithmetic  2.35 us (1%)
    pallas_call x1, Pallas kernels, per_device(): pl.pallas_call(functools.partial(attend_kernel, peers), out_shape=(jax.Sh...  108 us
    pallas_call x1, Pallas kernels, per_device(): pl.pallas_call(functools.partial(project_kernel, peers), out_shape=(jax.S...  75.9 us

profile of v3, /device:TPU:32, one launch (start us, length us, event | category | flops | bytes accessed | tf_op | source)
XLA Modules:
  0.0 192.0 jit_solution(15600634860734731304)
XLA Ops:
  0.6 0.0 copy-start
  0.6 0.0 copy-start.3
  0.7 0.0 copy-start.2
  0.7 1.3 divide_subtract_fusion
  2.0 0.1 multiply_cosine_fusion
  2.1 0.0 copy-done
  2.1 0.3 fusion.2
  2.4 0.0 copy-start.1
  2.4 0.2 copy.14
  2.5 0.1 reshape.33
  2.6 0.8 copy.15
  3.4 0.0 copy-done.3
  3.4 0.9 copy.16.label_ref
  4.3 0.0 copy-done.2
  4.3 0.0 copy-done.1
  4.4 1.0 pad_maximum_fusion.w_ref
  5.4 75.9 %project.1 = (bf16[512,384]{1,0:T(8,128)(2,1)}, bf16[640,768]{1,0:T(8,128)(2,1)}, s32[16,1,512]{2,1,0:T(1,128)}, f32[16,10,384]{2,1,0:T(8,128)}) custom-call(bf16[192,1920]{1,0:T(8,128)(2,1)} %pad_maximum_fusion.w_ref, bf16[512,3072]{1,0:T(8,128)(2,1)} %bitcast.15, bf16[128,3072]{1,0:T(8,128)(2,1)} %bitcast.21, s32[1,512]{1,0:T(1,128)} %bitcast.25, ...), custom_call_target="tpu_custom_call" | custom-call | tf_op jit(solution)/shard_map/project/pallas_call | solution.py:758
  81.3 108.0 %attend.1 = (f32[32,64]{1,0:T(8,128)}, f32[32,64]{1,0:T(8,128)}) custom-call(bf16[640,768]{1,0:T(8,128)(2,1)} %get-tuple-element.6.kv_ref, bf16[384,3072]{1,0:T(8,128)(2,1)} %out_w_ref.1, bf16[512,3072]{1,0:T(8,128)(2,1)} %bitcast.16, bf16[512,384]{1,0:T(8,128)(2,1)} %get-tuple-element.7.q_ref, s32[512,1]{1,0:T(8,128)} %copy.16.label_ref, ...), custom_call_target="tpu_custom_call" | custom-call | tf_op jit(solution)/shard_map/attend/pallas_call | solution.py:792
  189.3 1.3 copy.22
  190.6 1.3 copy.23
  (4 shorter events, 0.1 us)
Async XLA Ops:
  0.6 1.4 copy-start
  0.6 2.8 %copy-start.3 = (s32[512]{0:T(512)S(1)}, s32[512]{0:T(512)}, u32[]{:S(2)}) copy-start(s32[512]{0:T(512)} %param.13) | copy-start | bytes 6148
  0.7 3.6 %copy-start.2 = (bf16[192,2,384]{2,1,0:T(2,128)(2,1)S(1)}, bf16[192,2,384]{2,1,0:T(2,128)(2,1)}, u32[]{:S(2)}) copy-start(bf16[192,2,384]{2,1,0:T(2,128)(2,1)} %param.17) | copy-start | bytes 884740
  2.4 2.0 %copy-start.1 = (bf16[192,3,384]{2,0,1:T(8,128)(2,1)S(1)}, bf16[192,3,384]{2,0,1:T(8,128)(2,1)}, u32[]{:S(2)}) copy-start(bf16[192,3,384]{2,0,1:T(8,128)(2,1)} %param.16) | copy-start | bytes 1327108
